TPU v7x, 32 devices: a whole 2x2x4 slice. The times are simulated.
32 devices in a mesh: req: 8 (over y, x, core), tp: 4 (over z).
Axes of the slice: x: 2, y: 2, z: 4, core: 2. Of those that a mesh axis runs over, the one named last changes fastest.
Arguments:
- new_query: bfloat16 [1024, 2560], P('req', 'tp'), may hold values from -64 to 64
- new_keyval: bfloat16 [1024, 1280], P('req', 'tp'), may hold values from -24 to 24
- residual_in: bfloat16 [1024, 2560], P('req'), may hold values from -64 to 64
- leaf_cache: bfloat16 [128, 32, 1280], P('req', None, 'tp'), may hold values from -6 to 6
- leaf_length: int32 [128], P('req'), may hold values from 1 to 32
- new_counts: int32 [8, 16], P('req'), may hold values from 1 to 16, as said below
- request_mid: int32 [128], P('req'), may hold values from 0 to 5
- mid_root: int32 [6], replicated, may hold values from 0 to 1, as said below
- node_length: int32 [8], replicated, may hold values from 1 to 1744, as said below
- prefix_pool: bfloat16 [256, 16, 1280], P('req', None, 'tp'), may hold values from -6 to 6
- page_node: int32 [256], P('req'), may hold values from -1 to 7, as said below
- page_rank: int32 [256], P('req'), may hold values from 0 to 108, as said below
- out_weight: bfloat16 [2560, 2560], P('tp'), may hold values from -0.125 to 0.125
- norm_gain: bfloat16 [2560], replicated, may hold values from 0.5 to 1.5
- gate_weight: bfloat16 [2560, 3584], P(None, 'tp'), may hold values from -0.125 to 0.125
- up_weight: bfloat16 [2560, 3584], P(None, 'tp'), may hold values from -0.125 to 0.125
- down_weight: bfloat16 [3584, 2560], P('tp'), may hold values from -0.09375 to 0.09375
- next_gain: bfloat16 [2560], replicated, may hold values from 0.5 to 1.5
- query_weight: bfloat16 [2560, 2560], P(None, 'tp'), may hold values from -0.125 to 0.125
- keyval_weight: bfloat16 [2560, 1280], P(None, 'tp'), may hold values from -0.125 to 0.125
Outputs:
- attention: bfloat16 [1024, 2560], P('req', 'tp')
- residual_out: bfloat16 [1024, 2560], P(('req', 'tp'))
- next_query: bfloat16 [1024, 2560], P('req', 'tp')
- next_keyval: bfloat16 [1024, 1280], P('req', 'tp')
Inputs may be any that keep to these rules, and one draw needn't show every extreme that they name: `new_counts`: each row sums to 128 and holds one request of exactly 16 new tokens. `mid_root`: each root is the parent of 3 mid-level nodes. `node_length`: A node of k pages has more than 16 * (k - 1) and at most 16 * k prefix tokens; a node with the most pages has exactly 16 * k. `page_node`: every node owns one page or more; 32 pages are free (-1). `page_rank`: the k pages of a node carry the ranks 0 to k - 1, each once; free pages carry 0.
All inputs are finite; a program needn't handle non-finite values.
Results may differ from a plain program's by a relative error of at most 0.015.
Values may be sent and summed in bfloat16 or wider, within the bound.
No kernel may reach another device: no remote copies, remote signals or barrier semaphores. Data moves between devices by JAX's collectives and lax.ppermute only.
A program may use at most 128 MiB of HBM per device.

v0:
```python
import math
import jax
import jax.numpy as jnp
from jax import lax
from jax.sharding import PartitionSpec as P

HD = 80
MAXNEW = 16
ROOTS = 2
MIDS = 6
NODES = 8
MASKED = -1e30
EPSILON = 1e-05


def rms_scale(values_in, gain):
    values = values_in.astype(jnp.float32)
    scale = lax.rsqrt(jnp.mean(values * values, axis=-1, keepdims=True) + EPSILON)
    return (values * scale * gain.astype(jnp.float32)).astype(jnp.bfloat16)


def combine(first, second):
    top_first, total_first, sum_first = first
    top_second, total_second, sum_second = second
    top = jnp.maximum(top_first, top_second)
    factor_first = jnp.exp(top_first - top)
    factor_second = jnp.exp(top_second - top)
    total = total_first * factor_first + total_second * factor_second
    weighted = sum_first * factor_first[..., None] + sum_second * factor_second[..., None]
    return (top, total, weighted)


def attend(queries, keys, values, visible):
    scores = jnp.einsum("nkgd,mkd->nkgm", queries, keys, preferred_element_type=jnp.float32) * (
        1.0 / math.sqrt(HD)
    )
    shown = visible[:, None, None, :]
    scores = jnp.where(shown, scores, MASKED)
    top = jnp.max(scores, axis=-1)
    raised = jnp.where(shown, jnp.exp(scores - top[..., None]), 0.0)
    total = jnp.sum(raised, axis=-1)
    weighted = jnp.einsum(
        "nkgm,mkd->nkgd", raised.astype(jnp.bfloat16), values, preferred_element_type=jnp.float32
    )
    return (top, total, weighted)


def pool_split(pages_in, node_of_page, rank_of_page):
    page_count = pages_in.shape[0]
    page_size = pages_in.shape[1]
    flat = pages_in.reshape(page_count * page_size, pages_in.shape[2] // (2 * HD), 2, HD)
    key_node = jnp.repeat(node_of_page, page_size, total_repeat_length=page_count * page_size)
    key_place = (
        rank_of_page[:, None] * page_size + jnp.arange(page_size, dtype=jnp.int32)[None, :]
    ).reshape(page_count * page_size)
    return (flat[:, :, 0], flat[:, :, 1], key_node, key_place)


def shared_visible(token_info, key_node, key_place):
    root_hit = (key_node[None, :] == token_info[:, 0:1]) & (key_place[None, :] < token_info[:, 2:3])
    mid_hit = (key_node[None, :] == token_info[:, 1:2]) & (key_place[None, :] < token_info[:, 3:4])
    return root_hit | mid_hit


def token_tables(counts, request_mid, mid_root, node_length, row_count):
    requests = counts.shape[0]
    starts = jnp.cumsum(counts) - counts
    index = jnp.arange(row_count, dtype=jnp.int32)
    owner = jnp.sum((index[:, None] >= starts[None, :]).astype(jnp.int32), axis=1) - 1
    pick = (owner[:, None] == jnp.arange(requests, dtype=jnp.int32)[None, :]).astype(jnp.int32)
    offset = index - jnp.sum(pick * starts[None, :], axis=1)
    token_mid = jnp.sum(pick * request_mid[None, :], axis=1)
    mid_pick = (token_mid[:, None] == jnp.arange(MIDS, dtype=jnp.int32)[None, :]).astype(jnp.int32)
    token_root = jnp.sum(mid_pick * mid_root[None, :], axis=1)
    mid_node = token_mid + ROOTS
    node_ids = jnp.arange(NODES, dtype=jnp.int32)
    root_len = jnp.sum(
        (token_root[:, None] == node_ids[None, :]).astype(jnp.int32) * node_length[None, :], axis=1
    )
    mid_len = jnp.sum(
        (mid_node[:, None] == node_ids[None, :]).astype(jnp.int32) * node_length[None, :], axis=1
    )
    token_info = jnp.stack([token_root, mid_node, root_len, mid_len], axis=1)
    return (starts, owner, offset, token_info)


def local_part(
    new_query, new_keyval, leaf_cache, leaf_length, counts, starts, owner, offset, kv_local, group
):
    requests = counts.shape[0]
    leaf_slots = leaf_cache.shape[1]
    slot = jnp.arange(MAXNEW, dtype=jnp.int32)
    row_index = jnp.clip(starts[:, None] + slot[None, :], 0, new_query.shape[0] - 1)
    pad_query = new_query[row_index].reshape(requests, MAXNEW, kv_local, group, HD)
    pad_keyval = new_keyval[row_index]
    joined = jnp.concatenate([leaf_cache, pad_keyval], axis=1).reshape(
        requests, leaf_slots + MAXNEW, kv_local, 2, HD
    )
    leaf_ok = jnp.broadcast_to(
        jnp.arange(leaf_slots, dtype=jnp.int32)[None, None, :] < leaf_length[:, None, None],
        (requests, MAXNEW, leaf_slots),
    )
    causal = jnp.broadcast_to(
        slot[None, None, :] <= slot[None, :, None], (requests, MAXNEW, MAXNEW)
    )
    visible = jnp.concatenate([leaf_ok, causal], axis=2)
    part = jax.vmap(attend)(pad_query, joined[:, :, :, 0], joined[:, :, :, 1], visible)
    flat = owner * MAXNEW + offset
    return tuple((item.reshape((requests * MAXNEW,) + item.shape[2:])[flat] for item in part))


def visit_owners(new_query, token_info, prefix_pool, page_node, page_rank, kv_local, group):
    all_query, all_info = (
        lax.all_gather(new_query, "req", axis=0, tiled=True),
        lax.all_gather(token_info, "req", axis=0, tiled=True),
    )
    total_rows = all_query.shape[0]
    block = math.gcd(total_rows, 512)
    keys, values, key_node, key_place = pool_split(prefix_pool, page_node, page_rank)

    def owner_block(items):
        query_block, info_block = items
        heads = query_block.reshape(block, kv_local, group, HD)
        return attend(heads, keys, values, shared_visible(info_block, key_node, key_place))

    part = lax.map(
        owner_block,
        (
            all_query.reshape(total_rows // block, block, all_query.shape[1]),
            all_info.reshape(total_rows // block, block, 4),
        ),
    )
    holders = lax.axis_size("req")
    row_count = total_rows // holders
    part_top, part_total, part_sum = tuple(
        (item.reshape((holders, row_count) + item.shape[2:]) for item in part)
    )
    tops, totals, sums = (
        lax.all_to_all(part_top, "req", split_axis=0, concat_axis=0, tiled=True),
        lax.all_to_all(part_total, "req", split_axis=0, concat_axis=0, tiled=True),
        lax.all_to_all(part_sum, "req", split_axis=0, concat_axis=0, tiled=True),
    )
    top = jnp.max(tops, axis=0)
    factor = jnp.exp(tops - top[None])
    return (top, jnp.sum(totals * factor, axis=0), jnp.sum(sums * factor[..., None], axis=0))


def per_device(
    new_query,
    new_keyval,
    residual_in,
    leaf_cache,
    leaf_length,
    new_counts,
    request_mid,
    mid_root,
    node_length,
    prefix_pool,
    page_node,
    page_rank,
    out_weight,
    norm_gain,
    gate_weight,
    up_weight,
    down_weight,
    next_gain,
    query_weight,
    keyval_weight,
):
    row_count = new_query.shape[0]
    query_width = new_query.shape[1]
    keyval_width = new_keyval.shape[1]
    kv_local = keyval_width // (2 * HD)
    group = query_width // (kv_local * HD)
    counts = new_counts[0]
    starts, owner, offset, token_info = token_tables(
        counts, request_mid, mid_root, node_length, row_count
    )
    shared = visit_owners(new_query, token_info, prefix_pool, page_node, page_rank, kv_local, group)
    local = local_part(
        new_query,
        new_keyval,
        leaf_cache,
        leaf_length,
        counts,
        starts,
        owner,
        offset,
        kv_local,
        group,
    )
    top, total, weighted = combine(shared, local)
    attention = (weighted / total[..., None]).reshape(row_count, query_width).astype(jnp.bfloat16)
    share = row_count // lax.axis_size("tp")
    mine = lax.axis_index("tp") * share
    attn_proj = lax.psum(jnp.dot(attention, out_weight, preferred_element_type=jnp.float32), "tp")
    mixed = (residual_in.astype(jnp.float32) + attn_proj).astype(jnp.bfloat16)
    normed = rms_scale(mixed, norm_gain)
    gate = jnp.dot(normed, gate_weight, preferred_element_type=jnp.float32)
    upward = jnp.dot(normed, up_weight, preferred_element_type=jnp.float32)
    hidden = (jax.nn.silu(gate) * upward).astype(jnp.bfloat16)
    mlp_proj = lax.psum(jnp.dot(hidden, down_weight, preferred_element_type=jnp.float32), "tp")
    layer_rows = (mixed.astype(jnp.float32) + mlp_proj).astype(jnp.bfloat16)
    residual_out = lax.dynamic_slice_in_dim(layer_rows, mine, share, 0)
    final = rms_scale(layer_rows, next_gain)
    next_query = jnp.dot(final, query_weight, preferred_element_type=jnp.float32).astype(
        jnp.bfloat16
    )
    next_keyval = jnp.dot(final, keyval_weight, preferred_element_type=jnp.float32).astype(
        jnp.bfloat16
    )
    return (attention, residual_out, next_query, next_keyval)


def solution(mesh):
    in_specs = (
        P("req", "tp"),
        P("req", "tp"),
        P("req", None),
        P("req", None, "tp"),
        P("req"),
        P("req", None),
        P("req"),
        P(),
        P(),
        P("req", None, "tp"),
        P("req"),
        P("req"),
        P("tp", None),
        P(),
        P(None, "tp"),
        P(None, "tp"),
        P("tp", None),
        P(),
        P(None, "tp"),
        P(None, "tp"),
    )
    out_specs = (P("req", "tp"), P(("req", "tp"), None), P("req", "tp"), P("req", "tp"))
    return jax.shard_map(
        per_device, mesh=mesh, in_specs=in_specs, out_specs=out_specs, check_vma=False
    )
```

profile of v0, /device:TPU:0, one launch (start us, length us, event | category | flops | bytes accessed | tf_op | source)
XLA Modules:
  0.0 375.2 jit_solution(16658785647169500201)
XLA Ops:
  12.5 3.1 fusion.62
  20.8 11.4 %all_gather.6 = s32[1024,4]{0,1:T(4,128)} all-gather(s32[128,4]{0,1:T(4,128)S(1)} %pad_add_fusion.1), channel_id=1, replica_groups=mesh['req'=8,'tp'=4] {'req'}, dimensions={0}, use_global_device_ids=true | all-gather | bytes 18432 | tf_op jit(solution)/shard_map/all_gather | solution.py:115
  33.8 4.2 %compare_select_fusion.2 = (s32[512,1]{0,1:T(1,128)S(1)}, s32[512,1]{0,1:T(1,128)S(1)}) fusion(s32[]{:T(128)} %bitcast.29, s32[]{:T(128)} %bitcast.30, s32[]{:T(128)} %bitcast.31, s32[]{:T(128)} %bitcast.32, s32[]{:T(128)} %bitcast.33, s32[]{:T(128)} %bitcast.35, s32[]{:T(128)} %bitcast.34, s32[512,1]{0,1:T(1,128)S(1)} %bitcast.213, s32[512,1]{0,1:T(1,128)S(1)} %bitcast.212), kind=kLoop, calls=%fused_computation.105 | loop fusion | flops 7168 | bytes 8220 | tf_op jit(solution)/shard_map/jit(_take)/gather | solution.py:52
  38.6 16.0 %select_select_fusion = s32[512]{0:T(512)} fusion(pred[512]{0:T(512)(128)(4,1)S(1)} %get-tuple-element.200, pred[512]{0:T(512)(128)(4,1)S(1)} %get-tuple-element.199, pred[512]{0:T(512)(128)(4,1)S(1)} %get-tuple-element.198, pred[512]{0:T(512)(128)(4,1)S(1)} %get-tuple-element.197, pred[512]{0:T(512)(128)(4,1)S(1)} %get-tuple-element.196, ...), kind=kLoop, calls=%fused_computation.129 | loop fusion | flops 17408 | bytes 19060 | tf_op jit(solution)/shard_map/jit(_take)/select_n | solution.py:52
  54.6 100.4 %while.16 = (s32[]{:T(128)}, f32[2,512,2,4]{1,0,3,2:T(2,128)}, f32[2,512,2,4]{1,0,3,2:T(2,128)}, f32[2,512,2,4,80]{1,0,4,3,2:T(2,128)}, s32[512]{0:T(512)}, /*in...) while((s32[]{:T(128)}, f32[2,512,2,4]{1,0,3,2:T(2,128)}, ...), condition=%wide.region_9.10_spmd.clone, body=%wide.region_6.0_spmd.clone.sunk | while | flops 700178944 | bytes 71092600 | solution.py:126
  59.8 2.2 copy.193
  62.0 5.8 %bitcast_reduce_fusion.2 = (f32[512,2,4]{0,2,1:T(4,128)S(1)}, f32[2,512,4,512]{1,3,2,0:T(8,128)}) fusion(pred[512,512]{0,1:T(8,128)(4,1)S(1)} %and_or_fusion.2, bf16[512,2,4,80]{0,3,2,1:T(8,128)(2,1)} %bitcast.188, bf16[512,2,80]{0,2,1:T(8,128)(2,1)} %get-tuple-element.391), kind=kOutput, calls=%fused_computation.7.clone.1 | convolution fusion | flops 341831680 | bytes 9486336 | tf_op jit(solution)/shard_map/while/body/eval_jaxpr/nkgd,mkd->nkgm/dot_general | solution.py:34
  69.9 4.6 %fusion.85 = f32[512,2,4]{0,2,1:T(4,128)S(1)} fusion(f32[2,512,4,512]{1,3,2,0:T(8,128)} %get-tuple-element.359, f32[512,2,4]{0,2,1:T(4,128)S(1)} %get-tuple-element.358, pred[512,512]{0,1:T(8,128)(4,1)S(1)} %and_or_fusion.2), kind=kLoop, calls=%fused_computation.12.clone.1 | loop fusion | flops 10481664 | bytes 8683520 | tf_op jit(solution)/shard_map/while/body/eval_jaxpr/reduce_sum | solution.py:41
  75.8 2.3 fusion.86
  78.1 2.4 copy.196
  80.6 24.2 %dynamic_update_slice.19 = f32[2,512,2,4,80]{1,0,4,3,2:T(2,128)} dynamic-update-slice(f32[2,512,2,4,80]{1,0,4,3,2:T(2,128)} %get-tuple-element.375, f32[1,512,2,4,80]{1,0,4,3,2:T(1,128)} %copy.196, s32[]{:T(128)S(6)} %copy.204, s32[]{:T(128)} %constant.138.clone.1..sunk, s32[]{:T(128)} %constant.138.clone.1..sunk, s32[]{:T(128)} %constant.138.clone.1..sunk, s32[]{:T(128)} %constant.138.clone.1..sunk) | dynamic-update-slice | bytes 2621444 | tf_op jit(solution)/shard_map/while/body/jit(dynamic_update_index_in_dim)/dynamic_update_slice | solution.py:126
  112.2 5.8 %bitcast_reduce_fusion.2 = (f32[512,2,4]{0,2,1:T(4,128)S(1)}, f32[2,512,4,512]{1,3,2,0:T(8,128)}) fusion(pred[512,512]{0,1:T(8,128)(4,1)S(1)} %and_or_fusion.2, bf16[512,2,4,80]{0,3,2,1:T(8,128)(2,1)} %bitcast.188, bf16[512,2,80]{0,2,1:T(8,128)(2,1)} %get-tuple-element.391), kind=kOutput, calls=%fused_computation.7.clone.1 | convolution fusion | flops 341831680 | bytes 9486336 | tf_op jit(solution)/shard_map/while/body/eval_jaxpr/nkgd,mkd->nkgm/dot_general | solution.py:34
  120.1 4.6 %fusion.85 = f32[512,2,4]{0,2,1:T(4,128)S(1)} fusion(f32[2,512,4,512]{1,3,2,0:T(8,128)} %get-tuple-element.359, f32[512,2,4]{0,2,1:T(4,128)S(1)} %get-tuple-element.358, pred[512,512]{0,1:T(8,128)(4,1)S(1)} %and_or_fusion.2), kind=kLoop, calls=%fused_computation.12.clone.1 | loop fusion | flops 10481664 | bytes 8683520 | tf_op jit(solution)/shard_map/while/body/eval_jaxpr/reduce_sum | solution.py:41
  126.0 2.3 fusion.86
  128.3 2.4 copy.196
  130.8 24.2 %dynamic_update_slice.19 = f32[2,512,2,4,80]{1,0,4,3,2:T(2,128)} dynamic-update-slice(f32[2,512,2,4,80]{1,0,4,3,2:T(2,128)} %get-tuple-element.375, f32[1,512,2,4,80]{1,0,4,3,2:T(1,128)} %copy.196, s32[]{:T(128)S(6)} %copy.204, s32[]{:T(128)} %constant.138.clone.1..sunk, s32[]{:T(128)} %constant.138.clone.1..sunk, s32[]{:T(128)} %constant.138.clone.1..sunk, s32[]{:T(128)} %constant.138.clone.1..sunk) | dynamic-update-slice | bytes 2621444 | tf_op jit(solution)/shard_map/while/body/jit(dynamic_update_index_in_dim)/dynamic_update_slice | solution.py:126
  156.5 4.0 %all-to-all-start.1 = ((f32[8,128,2,4]{1,3,2,0:T(4,128)}), f32[8,128,2,4]{1,3,2,0:T(4,128)}, u32[]{:S(2)}, u32[]{:S(2)}) async-start(f32[8,128,2,4]{1,3,2,0:T(4,128)} %copy.135), calls=%async_computation.1 | async-start | bytes 65536 | tf_op jit(solution)/shard_map/all_to_all | solution.py:139
  165.4 4.1 %all-to-all-start.2 = ((f32[8,128,2,4]{1,3,2,0:T(4,128)}), f32[8,128,2,4]{1,3,2,0:T(4,128)S(1)}, u32[]{:S(2)}, u32[]{:S(2)}) async-start(f32[8,128,2,4]{1,3,2,0:T(4,128)} %copy.150), calls=%async_computation.2 | async-start | bytes 65536 | tf_op jit(solution)/shard_map/all_to_all | solution.py:140
  173.4 2.3 reshape.447
  175.7 3.7 reshape.446
  179.4 4.7 %reshape.442 = f32[8,128,2,4,80]{1,0,4,3,2:T(8,128)} reshape(f32[2,512,2,4,80]{1,0,4,3,2:T(2,128)} %get-tuple-element.70) | data formatting | bytes 5242880 | tf_op jit(solution)/shard_map/reshape | solution.py:136
  184.1 3.7 copy.133
  188.5 4.4 %all-to-all-start = ((f32[8,128,2,4,80]{1,4,3,2,0:T(8,128)}), f32[8,128,2,4,80]{1,4,3,2,0:T(8,128)}, u32[]{:S(2)}, u32[]{:S(2)}) async-start(f32[8,128,2,4,80]{1,4,3,2,0:T(8,128)} %copy.133), calls=%async_computation | async-start | bytes 5242880 | tf_op jit(solution)/shard_map/all_to_all | solution.py:141
  193.2 3.7 fusion.61
  203.0 2.9 gather_fusion.3
  209.7 2.5 fusion.30
  217.3 7.9 %all-to-all-done = f32[8,128,2,4,80]{1,4,3,2,0:T(8,128)} async-done(((f32[8,128,2,4,80]{1,4,3,2,0:T(8,128)}), f32[8,128,2,4,80]{1,4,3,2,0:T(8,128)}, u32[]{:S(2)}, u32[]{:S(2)}) %all-to-all-start) | async-done | bytes 2621472 | tf_op jit(solution)/shard_map/all_to_all | solution.py:141
  229.5 59.2 %all-reduce.3.cloned.1.call-done = f32[128,2560]{1,0:T(8,128)} async-done(((f32[128,2560]{1,0:T(8,128)}), f32[128,2560]{1,0:T(8,128)}) %all-reduce.3.cloned.1.call-update) | async-done | bytes 1310736 | tf_op jit(solution)/shard_map/psum | solution.py:196
  291.3 4.0 %fusion.45 = f32[128,896]{1,0:T(8,128)} fusion(bf16[2560,896]{1,0:T(8,128)(2,1)} %param.38, bf16[128,2560]{1,0:T(8,128)(2,1)S(1)} %get-tuple-element.228, f32[2560]{0:T(1024)S(1)} %convert_element_type.63, f32[128]{0:T(128)S(1)} %add_rsqrt_fusion.1), kind=kOutput, calls=%fused_computation.67 | convolution fusion | flops 588513280 | bytes 5712384 | tf_op jit(solution)/shard_map/dot_general | solution.py:199
  295.3 6.7 %fusion.29 = f32[128,2560]{1,0:T(8,128)} fusion(bf16[896,2560]{1,0:T(8,128)(2,1)} %param.40, bf16[2560,896]{1,0:T(8,128)(2,1)} %param.39, f32[128,896]{1,0:T(8,128)} %fusion.45, bf16[128,2560]{1,0:T(8,128)(2,1)} %copy-done.3, f32[2560]{0:T(1024)S(1)} %convert_element_type.63, f32[128]{0:T(128)S(1)} %add_rsqrt_fusion.1), kind=kOutput, calls=%fused_computation.50 | convolution fusion | flops 1176403968 | bytes 11610624 | tf_op jit(solution)/shard_map/dot_general | solution.py:202
  302.9 59.0 %all-reduce.5.cloned.1.call-done = f32[128,2560]{1,0:T(8,128)} async-done(((f32[128,2560]{1,0:T(8,128)}), f32[128,2560]{1,0:T(8,128)}) %all-reduce.5.cloned.1.call-update) | async-done | bytes 1310736 | tf_op jit(solution)/shard_map/psum | solution.py:202
  363.8 2.7 convolution_convert_fusion.1
  (152 shorter events, 69.6 us)
Async XLA Ops:
  7.2 220.2 %copy-start = (bf16[640,2560]{1,0:T(8,128)(2,1)S(1)}, bf16[640,2560]{1,0:T(8,128)(2,1)}, u32[]{:S(2)}) copy-start(bf16[640,2560]{1,0:T(8,128)(2,1)} %param.36) | copy-start | bytes 9830404
  7.2 26.5 %copy-start.11 = (s32[4,128]{1,0:T(4,128)S(1)}, s32[4,128]{1,0:T(4,128)}, u32[]{:S(2)}) copy-start(s32[4,128]{1,0:T(4,128)} %constant.143.clone.1) | copy-start | bytes 6148
  7.2 12.8 %copy-start.14 = (s32[16]{0:T(128)S(1)}, s32[16]{0:T(128)}, u32[]{:S(2)}) copy-start(s32[16]{0:T(128)} %param.30) | copy-start | bytes 196
  7.2 13.4 %copy-start.19 = (s32[6]{0:T(128)S(1)}, s32[6]{0:T(128)}, u32[]{:S(2)}) copy-start(s32[6]{0:T(128)} %param.31) | copy-start | bytes 76
  7.2 13.5 %copy-start.15 = (s32[8]{0:T(128)S(1)}, s32[8]{0:T(128)}, u32[]{:S(2)}) copy-start(s32[8]{0:T(128)} %param.32) | copy-start | bytes 100
  7.2 25.0 %copy-start.5 = (s32[32]{0:T(128)S(1)}, s32[32]{0:T(128)}, u32[]{:S(2)}) copy-start(s32[32]{0:T(128)} %param.34) | copy-start | bytes 388
  7.2 30.9 %copy-start.20 = (s32[32]{0:T(128)S(1)}, s32[32]{0:T(128)}, u32[]{:S(2)}) copy-start(s32[32]{0:T(128)} %param.35) | copy-start | bytes 388
  7.2 47.4 %all-gather.2.cloned.1.call-start = ((), (), s32[]{:S(2)}) async-start(), calls=%async_computation.3 | async-start | bytes 1474560 | tf_op jit(solution)/shard_map/all_gather | solution.py:114
  15.7 5.0 %copy-start.21 = (s32[128]{0:T(128)}, s32[128]{0:T(128)S(1)}, u32[]{:S(2)}) copy-start(s32[128]{0:T(128)S(1)} %convert_reduce_fusion) | copy-start | bytes 1540
  69.9 5.8 %copy-start.1 = (f32[2,512,4,512]{1,3,2,0:T(8,128)S(1)}, f32[2,512,4,512]{1,3,2,0:T(8,128)}, u32[]{:S(2)}) copy-start(f32[2,512,4,512]{1,3,2,0:T(8,128)} %get-tuple-element.359) | copy-start | bytes 25165828 | tf_op jit(solution)/shard_map/while
  69.9 5.8 %copy-start.7 = (bf16[512,2,80]{0,2,1:T(8,128)(2,1)S(1)}, bf16[512,2,80]{0,2,1:T(8,128)(2,1)}, u32[]{:S(2)}) copy-start(bf16[512,2,80]{0,2,1:T(8,128)(2,1)} %get-tuple-element.392) | copy-start | bytes 491524 | tf_op jit(solution)/shard_map/while
  78.1 2.4 copy-start.9
  80.6 24.2 %copy-start.10 = (f32[2,512,2,4]{1,0,3,2:T(2,128)}, f32[2,512,2,4]{1,0,3,2:T(2,128)S(1)}, u32[]{:S(2)}) copy-start(f32[2,512,2,4]{1,0,3,2:T(2,128)S(1)} %dynamic_update_slice.18) | copy-start | bytes 98308 | tf_op jit(solution)/shard_map/while
  120.1 5.8 %copy-start.1 = (f32[2,512,4,512]{1,3,2,0:T(8,128)S(1)}, f32[2,512,4,512]{1,3,2,0:T(8,128)}, u32[]{:S(2)}) copy-start(f32[2,512,4,512]{1,3,2,0:T(8,128)} %get-tuple-element.359) | copy-start | bytes 25165828 | tf_op jit(solution)/shard_map/while
  120.1 5.8 %copy-start.7 = (bf16[512,2,80]{0,2,1:T(8,128)(2,1)S(1)}, bf16[512,2,80]{0,2,1:T(8,128)(2,1)}, u32[]{:S(2)}) copy-start(bf16[512,2,80]{0,2,1:T(8,128)(2,1)} %get-tuple-element.392) | copy-start | bytes 491524 | tf_op jit(solution)/shard_map/while
  128.3 2.4 copy-start.9
  130.8 24.2 %copy-start.10 = (f32[2,512,2,4]{1,0,3,2:T(2,128)}, f32[2,512,2,4]{1,0,3,2:T(2,128)S(1)}, u32[]{:S(2)}) copy-start(f32[2,512,2,4]{1,0,3,2:T(2,128)S(1)} %dynamic_update_slice.18) | copy-start | bytes 98308 | tf_op jit(solution)/shard_map/while
  155.1 16.4 %copy-start.2 = (bf16[128,640]{1,0:T(8,128)(2,1)S(1)}, bf16[128,640]{1,0:T(8,128)(2,1)}, u32[]{:S(2)}) copy-start(bf16[128,640]{1,0:T(8,128)(2,1)} %param.24) | copy-start | bytes 491524
  156.5 8.8 %all-to-all-start.1 = ((f32[8,128,2,4]{1,3,2,0:T(4,128)}), f32[8,128,2,4]{1,3,2,0:T(4,128)}, u32[]{:S(2)}, u32[]{:S(2)}) async-start(f32[8,128,2,4]{1,3,2,0:T(4,128)} %copy.135), calls=%async_computation.1 | async-start | bytes 65536 | tf_op jit(solution)/shard_map/all_to_all | solution.py:139
  165.4 22.5 %all-to-all-start.2 = ((f32[8,128,2,4]{1,3,2,0:T(4,128)}), f32[8,128,2,4]{1,3,2,0:T(4,128)S(1)}, u32[]{:S(2)}, u32[]{:S(2)}) async-start(f32[8,128,2,4]{1,3,2,0:T(4,128)} %copy.150), calls=%async_computation.2 | async-start | bytes 65536 | tf_op jit(solution)/shard_map/all_to_all | solution.py:140
  187.9 5.1 %copy-start.16 = (s32[16]{0:T(128)S(1)}, s32[16]{0:T(128)}, u32[]{:S(2)}) copy-start(s32[16]{0:T(128)} %param.28) | copy-start | bytes 196
  188.5 36.7 %all-to-all-start = ((f32[8,128,2,4,80]{1,4,3,2,0:T(8,128)}), f32[8,128,2,4,80]{1,4,3,2,0:T(8,128)}, u32[]{:S(2)}, u32[]{:S(2)}) async-start(f32[8,128,2,4,80]{1,4,3,2,0:T(8,128)} %copy.133), calls=%async_computation | async-start | bytes 5242880 | tf_op jit(solution)/shard_map/all_to_all | solution.py:141
  192.9 95.8 %all-reduce.3.cloned.1.call-start = ((), (), s32[]{:S(2)}) async-start(), calls=%async_computation.4 | async-start | bytes 2621440 | tf_op jit(solution)/shard_map/psum | solution.py:196
  193.0 4.0 %copy-start.6 = (bf16[16,16,2,4,80]{4,3,2,1,0:T(4,128)(2,1)S(1)}, bf16[16,16,2,4,80]{4,3,2,1,0:T(4,128)(2,1)}, u32[]{:S(2)}) copy-start(bf16[16,16,2,4,80]{4,3,2,1,0:T(4,128)(2,1)} %reshape.447) | copy-start | bytes 983044
  201.2 1.8 copy-start.17
  201.2 1.8 copy-start.22
  225.2 2.1 copy-start.4
  227.3 2.1 copy-start.12
  229.2 132.7 %all-reduce.5.cloned.1.call-start = ((), (), s32[]{:S(2)}) async-start(), calls=%async_computation.5 | async-start | bytes 2621440 | tf_op jit(solution)/shard_map/psum | solution.py:202
  290.5 0.9 copy-start.3
  295.3 6.8 %copy-start.13 = (bf16[2560]{0:T(1024)(128)(2,1)S(1)}, bf16[2560]{0:T(1024)(128)(2,1)}, u32[]{:S(2)}) copy-start(bf16[2560]{0:T(1024)(128)(2,1)} %param.41) | copy-start | bytes 15364
  361.9 4.7 %copy-start.18 = (bf16[2560,640]{1,0:T(8,128)(2,1)S(1)}, bf16[2560,640]{1,0:T(8,128)(2,1)}, u32[]{:S(2)}) copy-start(bf16[2560,640]{1,0:T(8,128)(2,1)} %param.42) | copy-start | bytes 9830404
  (1 other events, 0.6 us)
Sparse Core Ops, SparseCore 0:
  10.0 27.2 all-gather.1
  229.3 59.3 all-reduce.2
  302.2 59.6 all-reduce.4
where the time goes:
time: 381 us; the launch traced here: 375 us
  waiting for transfers between devices  127 us (33%)
  local copies, waits for them, and re-layouts  125 us (33%)
  other arithmetic  49 us (13%)
  matrix products  36.3 us (10%)
  between operations  14.1 us (4%)
  starting transfers between devices  12.8 us (3%)
  blocking collectives  11.4 us (3%)
    psum x1, waiting for transfers between devices, per_device(): lax.psum(jnp.dot(attention, out_weight, preferred_element_type=jnp.float3...  59.2 us
    psum x1, waiting for transfers between devices, per_device(): lax.psum(jnp.dot(hidden, down_weight, preferred_element_type=jnp.float32)...  59 us
    dynamic_update_slice x12, local copies, waits for them, and re-layouts, visit_owners(): lax.map(owner_block, (all_query.reshape(total_rows // block, block, all_q...  57.6 us
    select_n x1, other arithmetic, pool_split(): jnp.repeat(node_of_page, page_size, total_repeat_length=page_count * page...  16 us
    dot_general x3, matrix products, attend(): jnp.einsum('nkgd,mkd->nkgm', queries, keys, preferred_element_type=jnp.fl...  13.1 us
    reduce_sum x3, other arithmetic, attend(): total = jnp.sum(raised, axis=-1)  11.8 us
    all_gather x1, blocking collectives, visit_owners(): lax.all_gather(token_info, 'req', axis=0, tiled=True)  11.4 us
    reshape x6, local copies, waits for them, and re-layouts, visit_owners(): item.reshape((holders, row_count) + item.shape[2:])  11.4 us
  transfers between devices with their start and end apart: 6, of which 3 were waited for; matrix products, arithmetic and copies ran while one was open for 22% of the time, Pallas kernels for 0%

commit v1 on v0

--- a/solution.py
+++ b/solution.py
@@ -193,7 +193,10 @@
     attention = (weighted / total[..., None]).reshape(row_count, query_width).astype(jnp.bfloat16)
     share = row_count // lax.axis_size("tp")
     mine = lax.axis_index("tp") * share
-    attn_proj = lax.psum(jnp.dot(attention, out_weight, preferred_element_type=jnp.float32), "tp")
+    attn_proj = jnp.sum(
+        lax.all_gather(jnp.dot(attention, out_weight, preferred_element_type=jnp.float32), "tp"),
+        axis=0,
+    )
     mixed = (residual_in.astype(jnp.float32) + attn_proj).astype(jnp.bfloat16)
     normed = rms_scale(mixed, norm_gain)
     gate = jnp.dot(normed, gate_weight, preferred_element_type=jnp.float32)

time: 381 us -> 422 us (1.11)
  waiting for transfers between devices: 127 us -> 164 us
    all_gather x0 -> x1, waiting for transfers between devices: none -> 97.3 us  [per_device(): lax.all_gather(jnp.dot(attention, out_weight, preferred_element_type=jnp....]
    psum x1 -> x0, waiting for transfers between devices: 59.2 us -> none  [per_device(): lax.psum(jnp.dot(attention, out_weight, preferred_element_type=jnp.float3...]
  transfers between devices with their start and end apart: 6 -> 6, of which waited for: 3 -> 3; matrix products, arithmetic and copies ran while one was open for 22% -> 20% of each run, Pallas kernels for 0% -> 0%
where the time goes in v1:
time: 422 us; the launch traced here: 416 us
  waiting for transfers between devices  164 us (39%)
  local copies, waits for them, and re-layouts  125 us (30%)
  other arithmetic  53.1 us (13%)
  matrix products  36.3 us (9%)
  between operations  14.1 us (3%)
  starting transfers between devices  12.8 us (3%)
  blocking collectives  11.4 us (3%)
    all_gather x1, waiting for transfers between devices, per_device(): lax.all_gather(jnp.dot(attention, out_weight, preferred_element_type=jnp....  97.3 us
    psum x1, waiting for transfers between devices, per_device(): lax.psum(jnp.dot(hidden, down_weight, preferred_element_type=jnp.float32)...  57.7 us
    dynamic_update_slice x12, local copies, waits for them, and re-layouts, visit_owners(): lax.map(owner_block, (all_query.reshape(total_rows // block, block, all_q...  57.6 us
    select_n x1, other arithmetic, pool_split(): jnp.repeat(node_of_page, page_size, total_repeat_length=page_count * page...  16 us
    dot_general x3, matrix products, attend(): jnp.einsum('nkgd,mkd->nkgm', queries, keys, preferred_element_type=jnp.fl...  13.1 us
    reduce_sum x3, other arithmetic, attend(): total = jnp.sum(raised, axis=-1)  11.8 us
    all_gather x1, blocking collectives, visit_owners(): lax.all_gather(token_info, 'req', axis=0, tiled=True)  11.4 us
    reshape x6, local copies, waits for them, and re-layouts, visit_owners(): item.reshape((holders, row_count) + item.shape[2:])  11.4 us
  transfers between devices with their start and end apart: 6, of which 3 were waited for; matrix products, arithmetic and copies ran while one was open for 20% of the time, Pallas kernels for 0%

profile of v1, /device:TPU:0, one launch (start us, length us, event | category | flops | bytes accessed | tf_op | source)
XLA Modules:
  0.0 416.1 jit_solution(8402770698400928321)
XLA Ops:
  12.5 3.1 fusion.62
  20.8 11.4 %all_gather.12 = s32[1024,4]{0,1:T(4,128)} all-gather(s32[128,4]{0,1:T(4,128)S(1)} %pad_add_fusion.1), channel_id=1, replica_groups=mesh['req'=8,'tp'=4] {'req'}, dimensions={0}, use_global_device_ids=true | all-gather | bytes 18432 | tf_op jit(solution)/shard_map/all_gather | solution.py:115
  33.8 4.2 %compare_select_fusion.2 = (s32[512,1]{0,1:T(1,128)S(1)}, s32[512,1]{0,1:T(1,128)S(1)}) fusion(s32[]{:T(128)} %bitcast.29, s32[]{:T(128)} %bitcast.30, s32[]{:T(128)} %bitcast.31, s32[]{:T(128)} %bitcast.32, s32[]{:T(128)} %bitcast.33, s32[]{:T(128)} %bitcast.35, s32[]{:T(128)} %bitcast.34, s32[512,1]{0,1:T(1,128)S(1)} %bitcast.215, s32[512,1]{0,1:T(1,128)S(1)} %bitcast.214), kind=kLoop, calls=%fused_computation.105 | loop fusion | flops 7168 | bytes 8220 | tf_op jit(solution)/shard_map/jit(_take)/gather | solution.py:52
  38.6 16.0 %select_select_fusion = s32[512]{0:T(512)} fusion(pred[512]{0:T(512)(128)(4,1)S(1)} %get-tuple-element.200, pred[512]{0:T(512)(128)(4,1)S(1)} %get-tuple-element.199, pred[512]{0:T(512)(128)(4,1)S(1)} %get-tuple-element.198, pred[512]{0:T(512)(128)(4,1)S(1)} %get-tuple-element.197, pred[512]{0:T(512)(128)(4,1)S(1)} %get-tuple-element.196, ...), kind=kLoop, calls=%fused_computation.129 | loop fusion | flops 17408 | bytes 19060 | tf_op jit(solution)/shard_map/jit(_take)/select_n | solution.py:52
  54.6 100.4 %while.16 = (s32[]{:T(128)}, f32[2,512,2,4]{1,0,3,2:T(2,128)}, f32[2,512,2,4]{1,0,3,2:T(2,128)}, f32[2,512,2,4,80]{1,0,4,3,2:T(2,128)}, s32[512]{0:T(512)}, /*in...) while((s32[]{:T(128)}, f32[2,512,2,4]{1,0,3,2:T(2,128)}, ...), condition=%wide.region_9.10_spmd.clone, body=%wide.region_6.0_spmd.clone.sunk | while | flops 700178944 | bytes 71092600 | solution.py:126
  62.0 5.8 %bitcast_reduce_fusion.2 = (f32[512,2,4]{0,2,1:T(4,128)S(1)}, f32[2,512,4,512]{1,3,2,0:T(8,128)}) fusion(pred[512,512]{0,1:T(8,128)(4,1)S(1)} %and_or_fusion.2, bf16[512,2,4,80]{0,3,2,1:T(8,128)(2,1)} %bitcast.189, bf16[512,2,80]{0,2,1:T(8,128)(2,1)} %get-tuple-element.391), kind=kOutput, calls=%fused_computation.7.clone.1 | convolution fusion | flops 341831680 | bytes 9486336 | tf_op jit(solution)/shard_map/while/body/eval_jaxpr/nkgd,mkd->nkgm/dot_general | solution.py:34
  69.9 4.6 %fusion.85 = f32[512,2,4]{0,2,1:T(4,128)S(1)} fusion(f32[2,512,4,512]{1,3,2,0:T(8,128)} %get-tuple-element.359, f32[512,2,4]{0,2,1:T(4,128)S(1)} %get-tuple-element.358, pred[512,512]{0,1:T(8,128)(4,1)S(1)} %and_or_fusion.2), kind=kLoop, calls=%fused_computation.12.clone.1 | loop fusion | flops 10481664 | bytes 8683520 | tf_op jit(solution)/shard_map/while/body/eval_jaxpr/reduce_sum | solution.py:41
  75.8 2.3 fusion.86
  78.1 2.4 copy.197
  80.6 24.2 %dynamic_update_slice.19 = f32[2,512,2,4,80]{1,0,4,3,2:T(2,128)} dynamic-update-slice(f32[2,512,2,4,80]{1,0,4,3,2:T(2,128)} %get-tuple-element.375, f32[1,512,2,4,80]{1,0,4,3,2:T(1,128)} %copy.197, s32[]{:T(128)S(6)} %copy.205, s32[]{:T(128)} %constant.138.clone.1..sunk, s32[]{:T(128)} %constant.138.clone.1..sunk, s32[]{:T(128)} %constant.138.clone.1..sunk, s32[]{:T(128)} %constant.138.clone.1..sunk) | dynamic-update-slice | bytes 2621444 | tf_op jit(solution)/shard_map/while/body/jit(dynamic_update_index_in_dim)/dynamic_update_slice | solution.py:126
  112.2 5.8 %bitcast_reduce_fusion.2 = (f32[512,2,4]{0,2,1:T(4,128)S(1)}, f32[2,512,4,512]{1,3,2,0:T(8,128)}) fusion(pred[512,512]{0,1:T(8,128)(4,1)S(1)} %and_or_fusion.2, bf16[512,2,4,80]{0,3,2,1:T(8,128)(2,1)} %bitcast.189, bf16[512,2,80]{0,2,1:T(8,128)(2,1)} %get-tuple-element.391), kind=kOutput, calls=%fused_computation.7.clone.1 | convolution fusion | flops 341831680 | bytes 9486336 | tf_op jit(solution)/shard_map/while/body/eval_jaxpr/nkgd,mkd->nkgm/dot_general | solution.py:34
  120.1 4.6 %fusion.85 = f32[512,2,4]{0,2,1:T(4,128)S(1)} fusion(f32[2,512,4,512]{1,3,2,0:T(8,128)} %get-tuple-element.359, f32[512,2,4]{0,2,1:T(4,128)S(1)} %get-tuple-element.358, pred[512,512]{0,1:T(8,128)(4,1)S(1)} %and_or_fusion.2), kind=kLoop, calls=%fused_computation.12.clone.1 | loop fusion | flops 10481664 | bytes 8683520 | tf_op jit(solution)/shard_map/while/body/eval_jaxpr/reduce_sum | solution.py:41
  126.0 2.3 fusion.86
  128.3 2.4 copy.197
  130.8 24.2 %dynamic_update_slice.19 = f32[2,512,2,4,80]{1,0,4,3,2:T(2,128)} dynamic-update-slice(f32[2,512,2,4,80]{1,0,4,3,2:T(2,128)} %get-tuple-element.375, f32[1,512,2,4,80]{1,0,4,3,2:T(1,128)} %copy.197, s32[]{:T(128)S(6)} %copy.205, s32[]{:T(128)} %constant.138.clone.1..sunk, s32[]{:T(128)} %constant.138.clone.1..sunk, s32[]{:T(128)} %constant.138.clone.1..sunk, s32[]{:T(128)} %constant.138.clone.1..sunk) | dynamic-update-slice | bytes 2621444 | tf_op jit(solution)/shard_map/while/body/jit(dynamic_update_index_in_dim)/dynamic_update_slice | solution.py:126
  156.5 4.0 all-to-all-start.1
  165.4 4.1 all-to-all-start.2
  173.4 2.3 reshape.447
  175.7 3.7 reshape.446
  179.4 4.7 %reshape.442 = f32[8,128,2,4,80]{1,0,4,3,2:T(8,128)} reshape(f32[2,512,2,4,80]{1,0,4,3,2:T(2,128)} %get-tuple-element.70) | data formatting | bytes 5242880 | tf_op jit(solution)/shard_map/reshape | solution.py:136
  184.1 3.7 copy.133
  188.5 4.4 %all-to-all-start = ((f32[8,128,2,4,80]{1,4,3,2,0:T(8,128)}), f32[8,128,2,4,80]{1,4,3,2,0:T(8,128)}, u32[]{:S(2)}, u32[]{:S(2)}) async-start(f32[8,128,2,4,80]{1,4,3,2,0:T(8,128)} %copy.133), calls=%async_computation | async-start | bytes 5242880 | tf_op jit(solution)/shard_map/all_to_all | solution.py:141
  193.2 3.7 fusion.61
  203.0 2.9 gather_fusion.3
  209.7 2.5 fusion.30
  217.3 7.9 %all-to-all-done = f32[8,128,2,4,80]{1,4,3,2,0:T(8,128)} async-done(((f32[8,128,2,4,80]{1,4,3,2,0:T(8,128)}), f32[8,128,2,4,80]{1,4,3,2,0:T(8,128)}, u32[]{:S(2)}, u32[]{:S(2)}) %all-to-all-start) | async-done | bytes 2621472 | tf_op jit(solution)/shard_map/all_to_all | solution.py:141
  229.5 97.3 %all-gather.6.cloned.1.call-done = f32[512,2560]{1,0:T(8,128)} async-done(((f32[128,2560]{1,0:T(8,128)}), f32[512,2560]{1,0:T(8,128)}) %all-gather.6.cloned.1.call-update) | async-done | bytes 5242896 | tf_op jit(solution)/shard_map/all_gather | solution.py:197
  326.8 4.1 reduce_sum.129
  333.5 4.0 fusion.45
  337.5 6.7 %fusion.29 = f32[128,2560]{1,0:T(8,128)} fusion(bf16[896,2560]{1,0:T(8,128)(2,1)} %param.40, bf16[2560,896]{1,0:T(8,128)(2,1)} %param.39, f32[128,896]{1,0:T(8,128)} %fusion.45, bf16[128,2560]{1,0:T(8,128)(2,1)} %copy-done.3, f32[2560]{0:T(1024)S(1)} %convert_element_type.63, f32[128]{0:T(128)S(1)} %add_rsqrt_fusion.1), kind=kOutput, calls=%fused_computation.50 | convolution fusion | flops 1176403968 | bytes 11610624 | tf_op jit(solution)/shard_map/dot_general | solution.py:205
  345.1 57.7 %all-reduce.2.cloned.1.call-done = f32[128,2560]{1,0:T(8,128)} async-done(((f32[128,2560]{1,0:T(8,128)}), f32[128,2560]{1,0:T(8,128)}) %all-reduce.2.cloned.1.call-update) | async-done | bytes 1310736 | tf_op jit(solution)/shard_map/psum | solution.py:205
  404.7 2.7 convolution_convert_fusion.1
  (153 shorter events, 71.8 us)
Async XLA Ops:
  7.2 220.2 %copy-start = (bf16[640,2560]{1,0:T(8,128)(2,1)S(1)}, bf16[640,2560]{1,0:T(8,128)(2,1)}, u32[]{:S(2)}) copy-start(bf16[640,2560]{1,0:T(8,128)(2,1)} %param.36) | copy-start | bytes 9830404
  7.2 26.5 %copy-start.11 = (s32[4,128]{1,0:T(4,128)S(1)}, s32[4,128]{1,0:T(4,128)}, u32[]{:S(2)}) copy-start(s32[4,128]{1,0:T(4,128)} %constant.143.clone.1) | copy-start | bytes 6148
  7.2 12.8 %copy-start.14 = (s32[16]{0:T(128)S(1)}, s32[16]{0:T(128)}, u32[]{:S(2)}) copy-start(s32[16]{0:T(128)} %param.30) | copy-start | bytes 196
  7.2 13.4 %copy-start.19 = (s32[6]{0:T(128)S(1)}, s32[6]{0:T(128)}, u32[]{:S(2)}) copy-start(s32[6]{0:T(128)} %param.31) | copy-start | bytes 76
  7.2 13.5 %copy-start.15 = (s32[8]{0:T(128)S(1)}, s32[8]{0:T(128)}, u32[]{:S(2)}) copy-start(s32[8]{0:T(128)} %param.32) | copy-start | bytes 100
  7.2 25.0 %copy-start.5 = (s32[32]{0:T(128)S(1)}, s32[32]{0:T(128)}, u32[]{:S(2)}) copy-start(s32[32]{0:T(128)} %param.34) | copy-start | bytes 388
  7.2 30.9 %copy-start.20 = (s32[32]{0:T(128)S(1)}, s32[32]{0:T(128)}, u32[]{:S(2)}) copy-start(s32[32]{0:T(128)} %param.35) | copy-start | bytes 388
  7.2 47.4 %all-gather.4.cloned.1.call-start = ((), (), s32[]{:S(2)}) async-start(), calls=%async_computation.3 | async-start | bytes 1474560 | tf_op jit(solution)/shard_map/all_gather | solution.py:114
  15.7 5.0 %copy-start.21 = (s32[128]{0:T(128)}, s32[128]{0:T(128)S(1)}, u32[]{:S(2)}) copy-start(s32[128]{0:T(128)S(1)} %convert_reduce_fusion) | copy-start | bytes 1540
  69.9 5.8 %copy-start.1 = (f32[2,512,4,512]{1,3,2,0:T(8,128)S(1)}, f32[2,512,4,512]{1,3,2,0:T(8,128)}, u32[]{:S(2)}) copy-start(f32[2,512,4,512]{1,3,2,0:T(8,128)} %get-tuple-element.359) | copy-start | bytes 25165828 | tf_op jit(solution)/shard_map/while
  69.9 5.8 %copy-start.7 = (bf16[512,2,80]{0,2,1:T(8,128)(2,1)S(1)}, bf16[512,2,80]{0,2,1:T(8,128)(2,1)}, u32[]{:S(2)}) copy-start(bf16[512,2,80]{0,2,1:T(8,128)(2,1)} %get-tuple-element.392) | copy-start | bytes 491524 | tf_op jit(solution)/shard_map/while
  78.1 2.4 copy-start.9
  80.6 24.2 %copy-start.10 = (f32[2,512,2,4]{1,0,3,2:T(2,128)}, f32[2,512,2,4]{1,0,3,2:T(2,128)S(1)}, u32[]{:S(2)}) copy-start(f32[2,512,2,4]{1,0,3,2:T(2,128)S(1)} %dynamic_update_slice.18) | copy-start | bytes 98308 | tf_op jit(solution)/shard_map/while
  120.1 5.8 %copy-start.1 = (f32[2,512,4,512]{1,3,2,0:T(8,128)S(1)}, f32[2,512,4,512]{1,3,2,0:T(8,128)}, u32[]{:S(2)}) copy-start(f32[2,512,4,512]{1,3,2,0:T(8,128)} %get-tuple-element.359) | copy-start | bytes 25165828 | tf_op jit(solution)/shard_map/while
  120.1 5.8 %copy-start.7 = (bf16[512,2,80]{0,2,1:T(8,128)(2,1)S(1)}, bf16[512,2,80]{0,2,1:T(8,128)(2,1)}, u32[]{:S(2)}) copy-start(bf16[512,2,80]{0,2,1:T(8,128)(2,1)} %get-tuple-element.392) | copy-start | bytes 491524 | tf_op jit(solution)/shard_map/while
  128.3 2.4 copy-start.9
  130.8 24.2 %copy-start.10 = (f32[2,512,2,4]{1,0,3,2:T(2,128)}, f32[2,512,2,4]{1,0,3,2:T(2,128)S(1)}, u32[]{:S(2)}) copy-start(f32[2,512,2,4]{1,0,3,2:T(2,128)S(1)} %dynamic_update_slice.18) | copy-start | bytes 98308 | tf_op jit(solution)/shard_map/while
  155.1 16.4 %copy-start.2 = (bf16[128,640]{1,0:T(8,128)(2,1)S(1)}, bf16[128,640]{1,0:T(8,128)(2,1)}, u32[]{:S(2)}) copy-start(bf16[128,640]{1,0:T(8,128)(2,1)} %param.24) | copy-start | bytes 491524
  156.5 8.8 %all-to-all-start.1 = ((f32[8,128,2,4]{1,3,2,0:T(4,128)}), f32[8,128,2,4]{1,3,2,0:T(4,128)}, u32[]{:S(2)}, u32[]{:S(2)}) async-start(f32[8,128,2,4]{1,3,2,0:T(4,128)} %copy.135), calls=%async_computation.1 | async-start | bytes 65536 | tf_op jit(solution)/shard_map/all_to_all | solution.py:139
  165.4 22.5 %all-to-all-start.2 = ((f32[8,128,2,4]{1,3,2,0:T(4,128)}), f32[8,128,2,4]{1,3,2,0:T(4,128)S(1)}, u32[]{:S(2)}, u32[]{:S(2)}) async-start(f32[8,128,2,4]{1,3,2,0:T(4,128)} %copy.150), calls=%async_computation.2 | async-start | bytes 65536 | tf_op jit(solution)/shard_map/all_to_all | solution.py:140
  187.9 5.1 %copy-start.16 = (s32[16]{0:T(128)S(1)}, s32[16]{0:T(128)}, u32[]{:S(2)}) copy-start(s32[16]{0:T(128)} %param.28) | copy-start | bytes 196
  188.5 36.7 %all-to-all-start = ((f32[8,128,2,4,80]{1,4,3,2,0:T(8,128)}), f32[8,128,2,4,80]{1,4,3,2,0:T(8,128)}, u32[]{:S(2)}, u32[]{:S(2)}) async-start(f32[8,128,2,4,80]{1,4,3,2,0:T(8,128)} %copy.133), calls=%async_computation | async-start | bytes 5242880 | tf_op jit(solution)/shard_map/all_to_all | solution.py:141
  192.9 133.9 %all-gather.6.cloned.1.call-start = ((), (), s32[]{:S(2)}) async-start(), calls=%async_computation.5 | async-start | bytes 6553600 | tf_op jit(solution)/shard_map/all_gather | solution.py:197
  193.0 4.0 copy-start.6
  201.2 1.8 copy-start.17
  201.2 1.8 copy-start.22
  225.2 2.1 copy-start.4
  227.3 2.1 copy-start.12
  229.2 173.6 %all-reduce.2.cloned.1.call-start = ((), (), s32[]{:S(2)}) async-start(), calls=%async_computation.4 | async-start | bytes 2621440 | tf_op jit(solution)/shard_map/psum | solution.py:205
  332.6 0.9 copy-start.3
  337.5 6.8 %copy-start.13 = (bf16[2560]{0:T(1024)(128)(2,1)S(1)}, bf16[2560]{0:T(1024)(128)(2,1)}, u32[]{:S(2)}) copy-start(bf16[2560]{0:T(1024)(128)(2,1)} %param.41) | copy-start | bytes 15364
  402.8 4.7 %copy-start.18 = (bf16[2560,640]{1,0:T(8,128)(2,1)S(1)}, bf16[2560,640]{1,0:T(8,128)(2,1)}, u32[]{:S(2)}) copy-start(bf16[2560,640]{1,0:T(8,128)(2,1)} %param.42) | copy-start | bytes 9830404
  (1 other events, 0.6 us)
Sparse Core Ops, SparseCore 0:
  10.0 27.2 all-gather.3
  229.3 97.4 all-gather.5
  344.4 58.3 all-reduce.1
